TPU v7x, 32 devices: a whole 2x2x4 slice. The times are simulated.
32 devices in a mesh: ctx: 4 (over z), dom: 2 (over y), rep: 4 (over x, core).
Axes of the slice: x: 2, y: 2, z: 4, core: 2. Of those that a mesh axis runs over, the one named last changes fastest.
Arguments:
- hidden: bfloat16 [4, 2, 512, 2048], P('rep', 'dom', 'ctx'), may hold values from -6 to 6
- bmat: bfloat16 [4, 2, 512, 128], P('rep', 'dom', 'ctx'), may hold values from -0.5 to 0.5
- cmat: bfloat16 [4, 2, 512, 128], P('rep', 'dom', 'ctx'), may hold values from -6 to 6
- tokens: int32 [4, 2, 512], P('rep', 'dom', 'ctx'), may hold values from 0 to 3
- table: float32 [4, 128], replicated, may hold values from -0.5 to 0.5
- step_size: float32 [4, 2, 512, 16], P('rep', 'dom', 'ctx'), may hold values from 0.005 to 0.05
- log_decay: float32 [4, 2, 512, 16], P('rep', 'dom', 'ctx'), may hold values from 0 to 1.5
- skip_gain: float32 [16], replicated, may hold values from 0.5 to 1.5
- prev_state: float32 [4, 2, 16, 128, 128], P('rep', 'dom', 'ctx'), may hold values from -0.5 to 0.5
- ancestors: int32 [4, 2], P('rep', 'dom'), may hold values from 0 to 1
- suffix_start: int32 [4], P('rep'), may hold values from 128 to 511
- cotangent: bfloat16 [4, 2, 512, 2048], P('rep', 'dom', 'ctx'), may hold values from -6 to 6
Outputs:
- mixed: bfloat16 [4, 2, 512, 2048], P('rep', 'dom', 'ctx')
- grad_hidden: bfloat16 [4, 2, 512, 2048], P('rep', 'dom', 'ctx')
- grad_bmat: bfloat16 [4, 2, 512, 128], P('rep', 'dom', 'ctx')
- grad_cmat: bfloat16 [4, 2, 512, 128], P('rep', 'dom', 'ctx')
- grad_table: float32 [4, 128], replicated
- grad_skip: float32 [16], replicated
All inputs are finite; a program needn't handle non-finite values.
Results may differ from a plain program's by a relative error of at most 0.008.
Values sent between devices are 32-bit elements; how exact they have to be, the bound alone decides.
No kernel may reach another device: no remote copies, remote signals or barrier semaphores. Data moves between devices by JAX's collectives and lax.ppermute only.
A program may use at most 192 MiB of HBM per device.

v0:
```python
import math
import jax
import jax.numpy as jnp
from jax import lax
from jax.sharding import PartitionSpec as P


def carried_in(value, axis, join, neutral, backward):
    count, mine = (lax.axis_size(axis), lax.axis_index(axis))
    pieces = jax.tree.map(lambda part: lax.all_gather(part, axis), value)
    if backward:
        pieces = jax.tree.map(lambda part: part[::-1], pieces)
        mine = count - 1 - mine
    running = jax.tree.map(
        lambda part, zero: jnp.full_like(part, 0) + jnp.asarray(zero, part.dtype), value, neutral
    )

    def turn(position, running):
        longer = join(running, jax.tree.map(lambda part: part[position], pieces))
        return jax.tree.map(lambda new, old: jnp.where(position < mine, new, old), longer, running)

    return lax.fori_loop(0, count - 1, turn, running)


def weigh(factor, values):
    return (factor[:, :, None] * values.astype(jnp.float32)).astype(jnp.bfloat16)


def block_terms(hidden_rows, writer, reader, step_rows, rate_rows, grad_rows):
    cumulative = jnp.cumsum(rate_rows, axis=0)
    totals = cumulative[-1]
    scaled = (step_rows[:, :, None] * hidden_rows.astype(jnp.float32)).astype(jnp.bfloat16)
    inner_dot = jnp.einsum("tn,sn->ts", reader, writer, preferred_element_type=jnp.float32)
    across = cumulative.T
    kernel = jnp.exp(-jnp.abs(across[:, :, None] - across[:, None, :]))
    weights = (kernel * inner_dot[None]).astype(jnp.bfloat16)
    mixed_in = jnp.einsum("hts,shp->thp", weights, scaled, preferred_element_type=jnp.float32)
    back_in = jnp.einsum("hts,thp->shp", weights, grad_rows, preferred_element_type=jnp.float32)
    paired = jnp.einsum("thp,shp->hts", grad_rows, scaled, preferred_element_type=jnp.float32)
    crossed = jnp.sum(kernel * paired, axis=0).astype(jnp.bfloat16)
    reader_in = jnp.einsum("ts,sn->tn", crossed, writer, preferred_element_type=jnp.float32)
    writer_in = jnp.einsum("ts,tn->sn", crossed, reader, preferred_element_type=jnp.float32)
    rising = jnp.exp(-cumulative)
    falling = jnp.exp(-(totals[None] - cumulative))
    state_end = jnp.einsum(
        "shp,sn->hpn", weigh(falling, scaled), writer, preferred_element_type=jnp.float32
    )
    state_begin = jnp.einsum(
        "shp,sn->hpn", weigh(rising, scaled), writer, preferred_element_type=jnp.float32
    )
    grad_end = jnp.einsum(
        "thp,tn->hpn", weigh(falling, grad_rows), reader, preferred_element_type=jnp.float32
    )
    grad_begin = jnp.einsum(
        "thp,tn->hpn", weigh(rising, grad_rows), reader, preferred_element_type=jnp.float32
    )
    decays = jnp.exp(-totals)
    return (
        mixed_in,
        back_in,
        reader_in,
        writer_in,
        rising,
        falling,
        scaled,
        decays,
        state_end,
        state_begin,
        grad_end,
        grad_begin,
    )


def finish(
    hidden_rows,
    writer,
    reader,
    step_rows,
    grad_rows,
    skip_gain,
    block_out,
    state_in,
    state_back,
    grad_in,
    grad_back,
):
    mixed_in, back_in, reader_in, writer_in, rising, falling, scaled = block_out
    state_in = state_in.astype(jnp.bfloat16)
    state_back = state_back.astype(jnp.bfloat16)
    grad_in = grad_in.astype(jnp.bfloat16)
    grad_back = grad_back.astype(jnp.bfloat16)
    rise = rising[:, :, None]
    fall = falling[:, :, None]
    mixed = (
        mixed_in
        + rise * jnp.einsum("hpn,tn->thp", state_in, reader, preferred_element_type=jnp.float32)
        + fall * jnp.einsum("hpn,tn->thp", state_back, reader, preferred_element_type=jnp.float32)
        + skip_gain[None, :, None] * hidden_rows.astype(jnp.float32)
    )
    back = (
        back_in
        + rise * jnp.einsum("hpn,sn->shp", grad_in, writer, preferred_element_type=jnp.float32)
        + fall * jnp.einsum("hpn,sn->shp", grad_back, writer, preferred_element_type=jnp.float32)
    )
    grad_hidden = step_rows[:, :, None] * back + skip_gain[None, :, None] * grad_rows.astype(
        jnp.float32
    )
    grad_reader = reader_in + jnp.sum(
        rise * jnp.einsum("thp,hpn->thn", grad_rows, state_in, preferred_element_type=jnp.float32)
        + fall
        * jnp.einsum("thp,hpn->thn", grad_rows, state_back, preferred_element_type=jnp.float32),
        axis=1,
    )
    grad_writer = writer_in + jnp.sum(
        rise * jnp.einsum("shp,hpn->shn", scaled, grad_in, preferred_element_type=jnp.float32)
        + fall * jnp.einsum("shp,hpn->shn", scaled, grad_back, preferred_element_type=jnp.float32),
        axis=1,
    )
    return (
        mixed.astype(jnp.bfloat16),
        grad_hidden.astype(jnp.bfloat16),
        grad_reader.astype(jnp.bfloat16),
        grad_writer,
    )


def chain_pair(earlier, latter):
    return (earlier[0] * latter[0], earlier[1] * latter[0][:, :, None, None] + latter[1])


def per_device(
    hidden,
    bmat,
    cmat,
    tokens,
    table,
    step_size,
    log_decay,
    skip_gain,
    prev_state,
    ancestors,
    suffix_start,
    cotangent,
):
    prompt_count, part_count, length, feature_dim = hidden.shape
    pair_count = prompt_count * part_count
    head_count = skip_gain.shape[0]
    head_dim = feature_dim // head_count
    state_dim = bmat.shape[3]
    vocab_size = table.shape[0]
    onehot = (tokens[..., None] == jnp.arange(vocab_size)[None, None, None, :]).astype(jnp.float32)
    looked = jnp.einsum("rplv,vn->rpln", onehot, table, precision=lax.Precision.HIGHEST)
    writer_all = (bmat.astype(jnp.float32) + looked).astype(jnp.bfloat16)
    symbol_site_indices = lax.axis_index("ctx") * length + jnp.arange(length)
    live_rows = symbol_site_indices[None, :] < suffix_start[:, None]
    grad_all = jnp.where(live_rows[:, None, :, None], cotangent, jnp.zeros_like(cotangent))
    shard_part = lax.all_gather(prev_state, "dom", axis=1, tiled=True)
    owners = jnp.arange(shard_part.shape[1])
    chosen = (ancestors[:, :, None] == owners[None, None, :]).astype(jnp.float32)
    chosen_heads = jnp.einsum(
        "rpk,rkhdn->rphdn", chosen, shard_part, precision=lax.Precision.HIGHEST
    )
    begin_state = lax.all_gather(chosen_heads, "ctx", axis=2, tiled=True).reshape(
        pair_count, head_count, head_dim, state_dim
    )
    hidden_rows = hidden.reshape(pair_count, length, head_count, head_dim)
    grad_rows = grad_all.reshape(pair_count, length, head_count, head_dim)
    writer = writer_all.reshape(pair_count, length, state_dim)
    reader = cmat.reshape(pair_count, length, state_dim)
    step_rows = step_size.reshape(pair_count, length, head_count)
    rate_rows = log_decay.reshape(pair_count, length, head_count)
    block_out = jax.vmap(block_terms)(hidden_rows, writer, reader, step_rows, rate_rows, grad_rows)
    decays, state_end, state_begin, grad_end, grad_begin = block_out[7:]
    at_first = jnp.where(lax.axis_index("ctx") == 0, 1.0, 0.0)
    seeded = state_end + at_first * decays[:, :, None, None] * begin_state
    unit_decay = jnp.ones_like(decays)
    zero_state = jnp.zeros_like(state_end)
    state_in = carried_in((decays, seeded), "ctx", chain_pair, (unit_decay, zero_state), False)[1]
    state_back = carried_in(
        (decays, state_begin), "ctx", chain_pair, (unit_decay, zero_state), True
    )[1]
    grad_in = carried_in((decays, grad_end), "ctx", chain_pair, (unit_decay, zero_state), False)[1]
    grad_back = carried_in((decays, grad_begin), "ctx", chain_pair, (unit_decay, zero_state), True)[
        1
    ]
    state_in = state_in + at_first * begin_state
    results = jax.vmap(finish, in_axes=(0, 0, 0, 0, 0, None, 0, 0, 0, 0, 0))(
        hidden_rows,
        writer,
        reader,
        step_rows,
        grad_rows,
        skip_gain,
        block_out[:7],
        state_in,
        state_back,
        grad_in,
        grad_back,
    )
    mixed = results[0].reshape(hidden.shape)
    grad_hidden = results[1].reshape(hidden.shape)
    grad_cmat = results[2].reshape(cmat.shape)
    grad_writer = results[3]
    total_rows = (
        pair_count * length * lax.axis_size("ctx") * lax.axis_size("dom") * lax.axis_size("rep")
    )
    writer_scale = 1.0 / math.sqrt(head_count * head_dim)
    total_scale = 1.0 / math.sqrt(total_rows)
    grad_bmat = (grad_writer * writer_scale).astype(jnp.bfloat16).reshape(bmat.shape)
    table_part = jnp.einsum(
        "clv,cln->vn",
        onehot.reshape(pair_count, length, vocab_size),
        grad_writer,
        precision=lax.Precision.HIGHEST,
    ) * (writer_scale * total_scale)
    skip_part = jnp.einsum(
        "clhp,clhp->h", hidden_rows, grad_rows, preferred_element_type=jnp.float32
    ) * (total_scale / math.sqrt(head_dim))
    grad_table, grad_skip = lax.psum((table_part, skip_part), ("ctx", "dom", "rep"))
    return (mixed, grad_hidden, grad_bmat, grad_cmat, grad_table, grad_skip)


def solution(mesh):
    return jax.shard_map(
        per_device,
        mesh=mesh,
        in_specs=(
            P("rep", "dom", "ctx", None),
            P("rep", "dom", "ctx", None),
            P("rep", "dom", "ctx", None),
            P("rep", "dom", "ctx"),
            P(),
            P("rep", "dom", "ctx", None),
            P("rep", "dom", "ctx", None),
            P(),
            P("rep", "dom", "ctx", None, None),
            P("rep", "dom"),
            P("rep"),
            P("rep", "dom", "ctx", None),
        ),
        out_specs=(
            P("rep", "dom", "ctx", None),
            P("rep", "dom", "ctx", None),
            P("rep", "dom", "ctx", None),
            P("rep", "dom", "ctx", None),
            P(),
            P(),
        ),
        check_vma=False,
    )
```

profile of v0, /device:TPU:0, one launch (start us, length us, event | category | flops | bytes accessed | tf_op | source)
XLA Modules:
  0.0 392.6 jit_solution(15929040369824743849)
XLA Ops:
  7.2 10.2 %all_gather.41 = f32[1,2,4,128,128]{4,3,2,0,1:T(8,128)S(1)} all-gather(f32[1,1,4,128,128]{4,3,2,0,1:T(8,128)} %bitcast.289), channel_id=1, replica_groups=mesh['ctx'=4,'dom'=2,'rep'=4] {'dom'}, dimensions={1}, use_global_device_ids=true | all-gather | bytes 786432 | tf_op jit(solution)/shard_map/all_gather | solution.py:157
  18.1 2.0 fusion.43
  20.2 0.8 copy.92
  21.4 0.3 copy.103
  21.7 1.1 mul.342
  22.8 1.6 copy.99
  24.5 1.3 mul.337.clone
  25.8 2.4 mul.344
  28.9 3.0 fusion.32
  31.9 1.4 copy.141
  33.3 0.2 fusion.29
  33.5 1.3 fusion.64
  34.9 1.3 copy.143
  36.2 1.3 fusion.56
  37.5 0.3 copy.142
  37.8 1.3 fusion.58
  39.2 1.1 fusion.81
  40.5 0.3 copy.140
  41.1 8.6 %all-gather.11.cloned.1.call-done = f32[16,128,128]{2,1,0:T(8,128)} async-done(((f32[4,128,128]{2,1,0:T(8,128)}), f32[16,128,128]{2,1,0:T(8,128)}) %all-gather.11.cloned.1.call-update) | async-done | bytes 1048592 | tf_op jit(solution)/shard_map/all_gather | solution.py:163
  49.6 2.5 convolution_add_fusion
  52.2 0.4 fusion.34
  52.5 2.2 copy.106
  54.8 9.5 %all_gather.40 = f32[4,1,16]{2,1,0:T(1,128)S(1)} all-gather(f32[1,1,16]{2,1,0:T(1,128)S(1)} %get-tuple-element.554), channel_id=1, replica_groups=mesh['ctx'=4,'dom'=2,'rep'=4] {'ctx'}, dimensions={0}, use_global_device_ids=true | all-gather | bytes 320 | tf_op jit(solution)/shard_map/all_gather | solution.py:10
  64.5 2.5 copy.114
  67.0 1.9 fusion.27
  68.9 62.6 %all-gather.15.cloned.1.call-done = f32[64,128,128]{2,1,0:T(8,128)} async-done(((f32[16,128,128]{2,1,0:T(8,128)}), f32[64,128,128]{2,1,0:T(8,128)}) %all-gather.15.cloned.1.call-update) | async-done | bytes 4194320 | tf_op jit(solution)/shard_map/all_gather | solution.py:10
  131.5 4.6 %rev.11 = f32[4,1,16,128,128]{4,3,2,1,0:T(8,128)} reverse(f32[4,1,16,128,128]{4,3,2,1,0:T(8,128)} %bitcast.277), dimensions={0} | reverse | bytes 8388608 | tf_op jit(solution)/shard_map/rev | solution.py:12
  136.1 76.3 %all-gather.19.cloned.1.call-done = f32[64,128,128]{2,1,0:T(8,128)} async-done(((f32[16,128,128]{2,1,0:T(8,128)}), f32[64,128,128]{2,1,0:T(8,128)}) %all-gather.19.cloned.1.call-update) | async-done | bytes 4194320 | tf_op jit(solution)/shard_map/all_gather | solution.py:10
  212.4 4.7 %rev.12 = f32[4,1,16,128,128]{4,3,2,1,0:T(8,128)} reverse(f32[4,1,16,128,128]{4,3,2,1,0:T(8,128)} %bitcast.278), dimensions={0} | reverse | bytes 8388608 | tf_op jit(solution)/shard_map/rev | solution.py:12
  217.0 4.6 %while.59 = (s32[]{:T(128)}, f32[1,16,128,128]{3,2,1,0:T(8,128)S(1)}, s32[]{:T(128)}, f32[4,1,16]{2,1,0:T(1,128)S(1)}, f32[4,1,16,128,128]{4,3,2,1,0:T(8,128)}, /*index=5*/s32[]{:T(128)}, s32[]{:T(128)}) while((s32[]{:T(128)}, f32[1,16,128,128]{3,2,1,0:T(8,128)S(1)}, s32[]{:T(128)}, f32[4,1,16]{2,1,0:T(1,128)S(1)}, ...), condition=%wide.region_8.9_spmd.clone, body=%wide.region_7.8_spmd.clone.sunk | while | flops 1048580 | bytes 3146025 | solution.py:22
  217.1 1.5 fusion.99
  218.5 1.6 fusion.99
  220.1 1.5 fusion.99
  221.7 1.3 fusion.8
  223.0 70.2 %all-gather.17.cloned.1.call-done = f32[64,128,128]{2,1,0:T(8,128)} async-done(((f32[16,128,128]{2,1,0:T(8,128)}), f32[64,128,128]{2,1,0:T(8,128)}) %all-gather.17.cloned.1.call-update) | async-done | bytes 4194320 | tf_op jit(solution)/shard_map/all_gather | solution.py:10
  293.1 4.5 %while.58 = (s32[]{:T(128)}, f32[1,16,128,128]{3,2,1,0:T(8,128)S(1)}, s32[]{:T(128)}, f32[4,1,16]{2,1,0:T(1,128)S(1)}, f32[4,1,16,128,128]{4,3,2,1,0:T(8,128)}, /*index=5*/s32[]{:T(128)}, s32[]{:T(128)}) while((s32[]{:T(128)}, f32[1,16,128,128]{3,2,1,0:T(8,128)S(1)}, s32[]{:T(128)}, f32[4,1,16]{2,1,0:T(1,128)S(1)}, ...), condition=%wide.region_6.7_spmd.clone, body=%wide.region_5.6_spmd.clone.sunk | while | flops 1048580 | bytes 3146025 | solution.py:22
  293.1 1.5 fusion.98
  294.6 1.5 fusion.98
  296.1 1.5 fusion.98
  297.6 0.3 fusion.9
  297.9 3.4 fusion.23
  301.3 2.1 copy.125
  303.4 1.7 fusion.19
  305.1 1.8 fusion.26
  307.2 0.3 convolution_multiply_fusion.3
  307.5 43.5 %all-reduce = (f32[4,128]{1,0:T(4,128)}, f32[16]{0:T(128)}) all-reduce(f32[4,128]{1,0:T(4,128)S(1)} %convolution_multiply_fusion.3, f32[16]{0:T(128)S(1)} %broadcast_multiply_fusion), channel_id=1, replica_groups=mesh['ctx'=4,'dom'=2,'rep'=4] {'ctx','dom','rep'}, use_global_device_ids=true, to_apply=%region_12.13 | all-reduce | flops 528 | bytes 4224 | tf_op jit(solution)/shard_map/psum | solution.py:219
  351.0 4.5 %while.57 = (s32[]{:T(128)}, f32[1,16,128,128]{3,2,1,0:T(8,128)S(1)}, s32[]{:T(128)}, f32[4,1,16]{2,1,0:T(1,128)S(1)}, f32[4,1,16,128,128]{4,3,2,1,0:T(8,128)}, /*index=5*/s32[]{:T(128)}, s32[]{:T(128)}) while((s32[]{:T(128)}, f32[1,16,128,128]{3,2,1,0:T(8,128)S(1)}, s32[]{:T(128)}, f32[4,1,16]{2,1,0:T(1,128)S(1)}, ...), condition=%wide.region_4.5_spmd.clone, body=%wide.region_3.4_spmd.clone.sunk | while | flops 1048580 | bytes 3146025 | solution.py:22
  351.0 1.5 fusion.97
  352.5 1.5 fusion.97
  354.0 1.5 fusion.97
  355.5 1.3 fusion.7
  356.8 0.6 fusion.55
  357.4 1.5 fusion.22
  359.0 15.9 %all-gather.13.cloned.1.call-done = f32[64,128,128]{2,1,0:T(8,128)} async-done(((f32[16,128,128]{2,1,0:T(8,128)}), f32[64,128,128]{2,1,0:T(8,128)}) %all-gather.13.cloned.1.call-update) | async-done | bytes 4194320 | tf_op jit(solution)/shard_map/all_gather | solution.py:10
  374.9 4.5 %while.56 = (s32[]{:T(128)}, f32[1,16,128,128]{3,2,1,0:T(8,128)S(1)}, s32[]{:T(128)}, f32[4,1,16]{2,1,0:T(1,128)S(1)}, f32[4,1,16,128,128]{4,3,2,1,0:T(8,128)}, /*index=5*/s32[]{:T(128)}, s32[]{:T(128)}) while((s32[]{:T(128)}, f32[1,16,128,128]{3,2,1,0:T(8,128)S(1)}, s32[]{:T(128)}, f32[4,1,16]{2,1,0:T(1,128)S(1)}, ...), condition=%wide.region_2.3_spmd.clone, body=%wide.region_1.2_spmd.clone.sunk | while | flops 1048580 | bytes 3146025 | solution.py:22
  374.9 1.5 fusion.96
  376.4 1.5 fusion.96
  377.9 1.5 fusion.96
  379.4 1.5 fusion.36
  380.9 0.3 fusion.5
  381.2 0.5 fusion.25
  381.8 0.8 fusion.31
  382.5 2.6 fusion.24
  385.1 1.0 copy.124
  (76 shorter events, 1.8 us)
Async XLA Ops:
  7.2 29.0 %copy-start = (bf16[1,1,128,128]{3,2,1,0:T(8,128)(2,1)S(1)}, bf16[1,1,128,128]{3,2,1,0:T(8,128)(2,1)}, u32[]{:S(2)}) copy-start(bf16[1,1,128,128]{3,2,1,0:T(8,128)(2,1)} %param.22) | copy-start | bytes 98308
  7.2 42.4 %all-gather.11.cloned.1.call-start = ((), (), s32[]{:S(2)}) async-start(), calls=%async_computation | async-start | bytes 1310720 | tf_op jit(solution)/shard_map/all_gather | solution.py:163
  7.2 17.1 %copy-start.11 = (f32[1,1,128,16]{2,3,1,0:T(8,128)S(1)}, f32[1,1,128,16]{2,3,1,0:T(8,128)}, u32[]{:S(2)}) copy-start(f32[1,1,128,16]{2,3,1,0:T(8,128)} %param.25) | copy-start | bytes 24580
  20.1 111.4 %all-gather.15.cloned.1.call-start = ((), (), s32[]{:S(2)}) async-start(), calls=%async_computation.2 | async-start | bytes 5242880 | tf_op jit(solution)/shard_map/all_gather | solution.py:10
  21.4 7.5 %copy-start.6 = (bf16[1,1,128,2048]{3,2,1,0:T(8,128)(2,1)S(1)}, bf16[1,1,128,2048]{3,2,1,0:T(8,128)(2,1)}, u32[]{:S(2)}) copy-start(bf16[1,1,128,2048]{3,2,1,0:T(8,128)(2,1)} %param.20) | copy-start | bytes 1572868
  21.4 7.5 %copy-start.8 = (bf16[1,1,128,2048]{3,2,1,0:T(8,128)(2,1)S(1)}, bf16[1,1,128,2048]{3,2,1,0:T(8,128)(2,1)}, u32[]{:S(2)}) copy-start(bf16[1,1,128,2048]{3,2,1,0:T(8,128)(2,1)} %param.31) | copy-start | bytes 1572868
  28.2 5.1 %copy-start.13 = (s32[1,1,128]{2,1,0:T(1,128)S(1)}, s32[1,1,128]{2,1,0:T(1,128)}, u32[]{:S(2)}) copy-start(s32[1,1,128]{2,1,0:T(1,128)} %param.23) | copy-start | bytes 1540
  28.2 5.1 %copy-start.14 = (bf16[1,1,128,128]{3,2,1,0:T(8,128)(2,1)S(1)}, bf16[1,1,128,128]{3,2,1,0:T(8,128)(2,1)}, u32[]{:S(2)}) copy-start(bf16[1,1,128,128]{3,2,1,0:T(8,128)(2,1)} %param.21) | copy-start | bytes 98308
  28.2 5.1 %copy-start.15 = (f32[4,128]{1,0:T(4,128)S(1)}, f32[4,128]{1,0:T(4,128)}, u32[]{:S(2)}) copy-start(f32[4,128]{1,0:T(4,128)} %param.24) | copy-start | bytes 6148
  31.9 5.7 %copy-start.10 = (bf16[1,1,128,2048]{3,2,1,0:T(8,128)(2,1)S(1)}, bf16[1,1,128,2048]{3,2,1,0:T(8,128)(2,1)}, u32[]{:S(2)}) copy-start(bf16[1,1,128,2048]{3,2,1,0:T(8,128)(2,1)} %get-tuple-element.551) | copy-start | bytes 1572868
  34.8 177.6 %all-gather.19.cloned.1.call-start = ((), (), s32[]{:S(2)}) async-start(), calls=%async_computation.4 | async-start | bytes 5242880 | tf_op jit(solution)/shard_map/all_gather | solution.py:10
  37.5 3.0 copy-start.9
  37.5 255.7 %all-gather.17.cloned.1.call-start = ((), (), s32[]{:S(2)}) async-start(), calls=%async_computation.3 | async-start | bytes 5242880 | tf_op jit(solution)/shard_map/all_gather | solution.py:10
  39.2 335.7 %all-gather.13.cloned.1.call-start = ((), (), s32[]{:S(2)}) async-start(), calls=%async_computation.1 | async-start | bytes 5242880 | tf_op jit(solution)/shard_map/all_gather | solution.py:10
  40.5 11.6 %copy-start.4 = (bf16[16,8,16,128]{3,2,1,0:T(8,128)(2,1)}, bf16[16,8,16,128]{3,2,1,0:T(8,128)(2,1)S(1)}, u32[]{:S(2)}) copy-start(bf16[16,8,16,128]{3,2,1,0:T(8,128)(2,1)S(1)} %copy.147) | copy-start | bytes 1572868
  40.9 11.2 %copy-start.2 = (bf16[16,8,16,128]{3,2,1,0:T(8,128)(2,1)}, bf16[16,8,16,128]{3,2,1,0:T(8,128)(2,1)S(1)}, u32[]{:S(2)}) copy-start(bf16[16,8,16,128]{3,2,1,0:T(8,128)(2,1)S(1)} %copy.146) | copy-start | bytes 1572868
  293.1 4.8 %copy-start.12 = (f32[16]{0:T(128)S(1)}, f32[16]{0:T(128)}, u32[]{:S(2)}) copy-start(f32[16]{0:T(128)} %param.27) | copy-start | bytes 196
  351.0 6.5 %copy-start.5 = (bf16[16,8,16,128]{3,2,1,0:T(8,128)(2,1)S(1)}, bf16[16,8,16,128]{3,2,1,0:T(8,128)(2,1)}, u32[]{:S(2)}) copy-start(bf16[16,8,16,128]{3,2,1,0:T(8,128)(2,1)} %copy-done.4) | copy-start | bytes 1572868
  355.5 19.4 %copy-start.1 = (f32[1,16,128,128]{3,2,1,0:T(8,128)S(1)}, f32[1,16,128,128]{3,2,1,0:T(8,128)}, u32[]{:S(2)}) copy-start(f32[1,16,128,128]{3,2,1,0:T(8,128)} %custom-call) | copy-start | bytes 3145732
  379.4 1.8 copy-start.7
  379.4 3.2 copy-start.3
Sparse Core Ops, SparseCore 0:
  20.2 29.3 all-gather.10
  51.2 80.2 all-gather.14
  133.1 79.2 all-gather.18
  213.8 79.2 all-gather.16
  294.6 80.2 all-gather.12
where the time goes:
time: 394 us; the launch traced here: 393 us
  waiting for transfers between devices  234 us (59%)
  blocking collectives  63.2 us (16%)
  local copies, waits for them, and re-layouts  28.8 us (7%)
  matrix products  26.5 us (7%)
  other arithmetic  24.6 us (6%)
  between operations  15.5 us (4%)
    all_gather x4, waiting for transfers between devices, carried_in(): pieces = jax.tree.map(lambda part: lax.all_gather(part, axis), value)  225 us
    psum x1, blocking collectives, per_device(): lax.psum((table_part, skip_part), ('ctx', 'dom', 'rep'))  43.5 us
    select_n x12, other arithmetic, turn(): jnp.where(position < mine, new, old)  17.7 us
    all_gather x1, blocking collectives, per_device(): shard_part = lax.all_gather(prev_state, 'dom', axis=1, tiled=True)  10.2 us
    all_gather x1, blocking collectives, carried_in(): pieces = jax.tree.map(lambda part: lax.all_gather(part, axis), value)  9.49 us
    rev x3, local copies, waits for them, and re-layouts, carried_in(): pieces = jax.tree.map(lambda part: part[::-1], pieces)  9.28 us
    all_gather x1, waiting for transfers between devices, per_device(): lax.all_gather(chosen_heads, 'ctx', axis=2, tiled=True)  8.56 us
  transfers between devices with their start and end apart: 5, of which 5 were waited for; matrix products, arithmetic and copies ran while one was open for 17% of the time, Pallas kernels for 0%

commit v1 on v0

--- a/solution.py
+++ b/solution.py
@@ -216,7 +216,7 @@
     skip_part = jnp.einsum(
         "clhp,clhp->h", hidden_rows, grad_rows, preferred_element_type=jnp.float32
     ) * (total_scale / math.sqrt(head_dim))
-    grad_table, grad_skip = lax.psum((table_part, skip_part), ("ctx", "dom", "rep"))
+    grad_table, grad_skip = lax.psum(lax.psum((table_part, skip_part), "ctx"), ("dom", "rep"))
     return (mixed, grad_hidden, grad_bmat, grad_cmat, grad_table, grad_skip)
 
 

time: 394 us -> 392 us (level)
  waiting for transfers between devices: 234 us -> 255 us
  blocking collectives: 63.2 us -> 42.4 us
    all_gather x4, waiting for transfers between devices: 225 us -> 246 us  [carried_in(): pieces = jax.tree.map(lambda part: lax.all_gather(part, axis), value)]
    psum x1 -> x2, blocking collectives: 43.5 us -> 22.8 us  [the longest x1 13.5 us: per_device(): lax.psum(lax.psum((table_part, skip_part), 'ctx'), ('dom', 'rep'))]
where the time goes in v1:
time: 392 us; the launch traced here: 391 us
  waiting for transfers between devices  255 us (65%)
  blocking collectives  42.4 us (11%)
  local copies, waits for them, and re-layouts  27.9 us (7%)
  matrix products  25.3 us (6%)
  other arithmetic  24.6 us (6%)
  between operations  15.6 us (4%)
    all_gather x4, waiting for transfers between devices, carried_in(): pieces = jax.tree.map(lambda part: lax.all_gather(part, axis), value)  246 us
    select_n x12, other arithmetic, turn(): jnp.where(position < mine, new, old)  17.7 us
    psum x1, blocking collectives, per_device(): lax.psum(lax.psum((table_part, skip_part), 'ctx'), ('dom', 'rep'))  13.5 us
    all_gather x1, blocking collectives, per_device(): shard_part = lax.all_gather(prev_state, 'dom', axis=1, tiled=True)  10.2 us
    all_gather x1, blocking collectives, carried_in(): pieces = jax.tree.map(lambda part: lax.all_gather(part, axis), value)  9.39 us
    rev x3, local copies, waits for them, and re-layouts, carried_in(): pieces = jax.tree.map(lambda part: part[::-1], pieces)  9.28 us
    psum x1, blocking collectives, per_device(): lax.psum((table_part, skip_part), 'ctx')  9.24 us
    all_gather x1, waiting for transfers between devices, per_device(): lax.all_gather(chosen_heads, 'ctx', axis=2, tiled=True)  8.5 us
  transfers between devices with their start and end apart: 5, of which 5 were waited for; matrix products, arithmetic and copies ran while one was open for 17% of the time, Pallas kernels for 0%

profile of v1, /device:TPU:0, one launch (start us, length us, event | category | flops | bytes accessed | tf_op | source)
XLA Modules:
  0.0 390.9 jit_solution(2276945060931763780)
XLA Ops:
  7.2 10.2 %all_gather.41 = f32[1,2,4,128,128]{4,3,2,0,1:T(8,128)S(1)} all-gather(f32[1,1,4,128,128]{4,3,2,0,1:T(8,128)} %bitcast.289), channel_id=1, replica_groups=mesh['ctx'=4,'dom'=2,'rep'=4] {'dom'}, dimensions={1}, use_global_device_ids=true | all-gather | bytes 786432 | tf_op jit(solution)/shard_map/all_gather | solution.py:157
  18.1 2.0 fusion.43
  20.2 0.8 copy.92
  21.4 0.3 copy.99
  21.8 1.3 mul.337.clone
  23.2 1.4 mul.344
  24.6 1.0 mul.341
  25.6 2.6 copy.103
  28.9 3.0 fusion.32
  31.9 1.4 copy.141
  33.5 1.3 fusion.64
  34.9 1.4 copy.143
  36.3 1.3 fusion.56
  37.6 0.3 copy.142
  37.9 1.3 fusion.58
  39.3 0.3 copy.140
  39.7 1.1 fusion.81
  41.1 8.5 %all-gather.11.cloned.1.call-done = f32[16,128,128]{2,1,0:T(8,128)} async-done(((f32[4,128,128]{2,1,0:T(8,128)}), f32[16,128,128]{2,1,0:T(8,128)}) %all-gather.11.cloned.1.call-update) | async-done | bytes 1048592 | tf_op jit(solution)/shard_map/all_gather | solution.py:163
  49.6 2.5 convolution_add_fusion
  52.1 0.4 fusion.34
  52.5 1.2 copy.106
  53.7 9.4 %all_gather.40 = f32[4,1,16]{2,1,0:T(1,128)S(1)} all-gather(f32[1,1,16]{2,1,0:T(1,128)S(1)} %get-tuple-element.556), channel_id=1, replica_groups=mesh['ctx'=4,'dom'=2,'rep'=4] {'ctx'}, dimensions={0}, use_global_device_ids=true | all-gather | bytes 320 | tf_op jit(solution)/shard_map/all_gather | solution.py:10
  63.3 2.6 copy.114
  65.8 1.9 fusion.27
  67.8 63.7 %all-gather.15.cloned.1.call-done = f32[64,128,128]{2,1,0:T(8,128)} async-done(((f32[16,128,128]{2,1,0:T(8,128)}), f32[64,128,128]{2,1,0:T(8,128)}) %all-gather.15.cloned.1.call-update) | async-done | bytes 4194320 | tf_op jit(solution)/shard_map/all_gather | solution.py:10
  131.5 4.6 %rev.11 = f32[4,1,16,128,128]{4,3,2,1,0:T(8,128)} reverse(f32[4,1,16,128,128]{4,3,2,1,0:T(8,128)} %bitcast.277), dimensions={0} | reverse | bytes 8388608 | tf_op jit(solution)/shard_map/rev | solution.py:12
  136.1 76.3 %all-gather.19.cloned.1.call-done = f32[64,128,128]{2,1,0:T(8,128)} async-done(((f32[16,128,128]{2,1,0:T(8,128)}), f32[64,128,128]{2,1,0:T(8,128)}) %all-gather.19.cloned.1.call-update) | async-done | bytes 4194320 | tf_op jit(solution)/shard_map/all_gather | solution.py:10
  212.4 4.7 %rev.12 = f32[4,1,16,128,128]{4,3,2,1,0:T(8,128)} reverse(f32[4,1,16,128,128]{4,3,2,1,0:T(8,128)} %bitcast.278), dimensions={0} | reverse | bytes 8388608 | tf_op jit(solution)/shard_map/rev | solution.py:12
  217.0 4.6 %while.59 = (s32[]{:T(128)}, f32[1,16,128,128]{3,2,1,0:T(8,128)S(1)}, s32[]{:T(128)}, f32[4,1,16]{2,1,0:T(1,128)S(1)}, f32[4,1,16,128,128]{4,3,2,1,0:T(8,128)}, /*index=5*/s32[]{:T(128)}, s32[]{:T(128)}) while((s32[]{:T(128)}, f32[1,16,128,128]{3,2,1,0:T(8,128)S(1)}, s32[]{:T(128)}, f32[4,1,16]{2,1,0:T(1,128)S(1)}, ...), condition=%wide.region_8.9_spmd.clone, body=%wide.region_7.8_spmd.clone.sunk | while | flops 1048580 | bytes 3146033 | solution.py:22
  217.0 1.5 fusion.99
  218.5 1.6 fusion.99
  220.1 1.5 fusion.99
  221.7 1.3 fusion.8
  223.0 70.2 %all-gather.17.cloned.1.call-done = f32[64,128,128]{2,1,0:T(8,128)} async-done(((f32[16,128,128]{2,1,0:T(8,128)}), f32[64,128,128]{2,1,0:T(8,128)}) %all-gather.17.cloned.1.call-update) | async-done | bytes 4194320 | tf_op jit(solution)/shard_map/all_gather | solution.py:10
  293.1 4.5 %while.58 = (s32[]{:T(128)}, f32[1,16,128,128]{3,2,1,0:T(8,128)S(1)}, s32[]{:T(128)}, f32[4,1,16]{2,1,0:T(1,128)S(1)}, f32[4,1,16,128,128]{4,3,2,1,0:T(8,128)}, /*index=5*/s32[]{:T(128)}, s32[]{:T(128)}) while((s32[]{:T(128)}, f32[1,16,128,128]{3,2,1,0:T(8,128)S(1)}, s32[]{:T(128)}, f32[4,1,16]{2,1,0:T(1,128)S(1)}, ...), condition=%wide.region_6.7_spmd.clone, body=%wide.region_5.6_spmd.clone.sunk | while | flops 1048580 | bytes 3146033 | solution.py:22
  293.1 1.5 fusion.98
  294.6 1.5 fusion.98
  296.1 1.5 fusion.98
  297.6 0.3 fusion.9
  298.0 3.4 fusion.23
  301.3 2.1 copy.125
  303.4 1.7 fusion.19
  305.2 1.8 fusion.26
  307.3 0.3 convolution_multiply_fusion.3
  307.5 9.2 %all-reduce.1 = (f32[4,128]{1,0:T(4,128)S(1)}, f32[16]{0:T(128)S(1)}) all-reduce(f32[4,128]{1,0:T(4,128)S(1)} %convolution_multiply_fusion.3, f32[16]{0:T(128)S(1)} %broadcast_multiply_fusion), channel_id=1, replica_groups=mesh['ctx'=4,'dom'=2,'rep'=4] {'ctx'}, use_global_device_ids=true, to_apply=%region_12.13 | all-reduce | flops 528 | bytes 4224 | tf_op jit(solution)/shard_map/psum | solution.py:219
  316.8 13.5 %all-reduce = (f32[4,128]{1,0:T(4,128)}, f32[16]{0:T(128)}) all-reduce(f32[4,128]{1,0:T(4,128)S(1)} %get-tuple-element.548, f32[16]{0:T(128)S(1)} %get-tuple-element.549), channel_id=1, replica_groups=mesh['ctx'=4,'dom'=2,'rep'=4] {'dom','rep'}, use_global_device_ids=true, to_apply=%region_13.14 | all-reduce | flops 528 | bytes 4224 | tf_op jit(solution)/shard_map/psum | solution.py:219
  330.3 4.5 %while.57 = (s32[]{:T(128)}, f32[1,16,128,128]{3,2,1,0:T(8,128)S(1)}, s32[]{:T(128)}, f32[4,1,16]{2,1,0:T(1,128)S(1)}, f32[4,1,16,128,128]{4,3,2,1,0:T(8,128)}, /*index=5*/s32[]{:T(128)}, s32[]{:T(128)}) while((s32[]{:T(128)}, f32[1,16,128,128]{3,2,1,0:T(8,128)S(1)}, s32[]{:T(128)}, f32[4,1,16]{2,1,0:T(1,128)S(1)}, ...), condition=%wide.region_4.5_spmd.clone, body=%wide.region_3.4_spmd.clone.sunk | while | flops 1048580 | bytes 3146033 | solution.py:22
  330.3 1.5 fusion.97
  331.9 1.5 fusion.97
  333.4 1.5 fusion.97
  334.9 1.3 fusion.7
  336.2 0.6 fusion.55
  336.8 1.5 fusion.22
  338.3 35.8 %all-gather.13.cloned.1.call-done = f32[64,128,128]{2,1,0:T(8,128)} async-done(((f32[16,128,128]{2,1,0:T(8,128)}), f32[64,128,128]{2,1,0:T(8,128)}) %all-gather.13.cloned.1.call-update) | async-done | bytes 4194320 | tf_op jit(solution)/shard_map/all_gather | solution.py:10
  374.1 4.5 %while.56 = (s32[]{:T(128)}, f32[1,16,128,128]{3,2,1,0:T(8,128)S(1)}, s32[]{:T(128)}, f32[4,1,16]{2,1,0:T(1,128)S(1)}, f32[4,1,16,128,128]{4,3,2,1,0:T(8,128)}, /*index=5*/s32[]{:T(128)}, s32[]{:T(128)}) while((s32[]{:T(128)}, f32[1,16,128,128]{3,2,1,0:T(8,128)S(1)}, s32[]{:T(128)}, f32[4,1,16]{2,1,0:T(1,128)S(1)}, ...), condition=%wide.region_2.3_spmd.clone, body=%wide.region_1.2_spmd.clone.sunk | while | flops 1048580 | bytes 3146033 | solution.py:22
  374.1 1.5 fusion.96
  375.6 1.5 fusion.96
  377.1 1.5 fusion.96
  378.6 1.5 fusion.36
  380.1 0.3 fusion.5
  380.6 1.4 fusion.24
  382.0 1.0 copy.124
  383.0 0.5 fusion.25
  383.6 0.8 fusion.31
  (81 shorter events, 2.2 us)
Async XLA Ops:
  7.2 29.1 %copy-start = (bf16[1,1,128,128]{3,2,1,0:T(8,128)(2,1)S(1)}, bf16[1,1,128,128]{3,2,1,0:T(8,128)(2,1)}, u32[]{:S(2)}) copy-start(bf16[1,1,128,128]{3,2,1,0:T(8,128)(2,1)} %param.22) | copy-start | bytes 98308
  7.2 14.6 %copy-start.13 = (f32[1,1,128,16]{2,3,1,0:T(8,128)S(1)}, f32[1,1,128,16]{2,3,1,0:T(8,128)}, u32[]{:S(2)}) copy-start(f32[1,1,128,16]{2,3,1,0:T(8,128)} %param.25) | copy-start | bytes 24580
  7.2 42.4 %all-gather.11.cloned.1.call-start = ((), (), s32[]{:S(2)}) async-start(), calls=%async_computation | async-start | bytes 1310720 | tf_op jit(solution)/shard_map/all_gather | solution.py:163
  20.1 111.4 %all-gather.15.cloned.1.call-start = ((), (), s32[]{:S(2)}) async-start(), calls=%async_computation.2 | async-start | bytes 5242880 | tf_op jit(solution)/shard_map/all_gather | solution.py:10
  21.4 7.5 %copy-start.6 = (bf16[1,1,128,2048]{3,2,1,0:T(8,128)(2,1)S(1)}, bf16[1,1,128,2048]{3,2,1,0:T(8,128)(2,1)}, u32[]{:S(2)}) copy-start(bf16[1,1,128,2048]{3,2,1,0:T(8,128)(2,1)} %param.20) | copy-start | bytes 1572868
  21.4 7.5 %copy-start.10 = (bf16[1,1,128,2048]{3,2,1,0:T(8,128)(2,1)S(1)}, bf16[1,1,128,2048]{3,2,1,0:T(8,128)(2,1)}, u32[]{:S(2)}) copy-start(bf16[1,1,128,2048]{3,2,1,0:T(8,128)(2,1)} %param.31) | copy-start | bytes 1572868
  28.2 5.1 %copy-start.15 = (s32[1,1,128]{2,1,0:T(1,128)S(1)}, s32[1,1,128]{2,1,0:T(1,128)}, u32[]{:S(2)}) copy-start(s32[1,1,128]{2,1,0:T(1,128)} %param.23) | copy-start | bytes 1540
  28.2 5.1 %copy-start.16 = (bf16[1,1,128,128]{3,2,1,0:T(8,128)(2,1)S(1)}, bf16[1,1,128,128]{3,2,1,0:T(8,128)(2,1)}, u32[]{:S(2)}) copy-start(bf16[1,1,128,128]{3,2,1,0:T(8,128)(2,1)} %param.21) | copy-start | bytes 98308
  28.2 5.1 %copy-start.17 = (f32[4,128]{1,0:T(4,128)S(1)}, f32[4,128]{1,0:T(4,128)}, u32[]{:S(2)}) copy-start(f32[4,128]{1,0:T(4,128)} %param.24) | copy-start | bytes 6148
  31.9 5.7 %copy-start.12 = (bf16[1,1,128,2048]{3,2,1,0:T(8,128)(2,1)S(1)}, bf16[1,1,128,2048]{3,2,1,0:T(8,128)(2,1)}, u32[]{:S(2)}) copy-start(bf16[1,1,128,2048]{3,2,1,0:T(8,128)(2,1)} %get-tuple-element.553) | copy-start | bytes 1572868
  34.8 4.5 %copy-start.11 = (bf16[1,1,128,2048]{3,2,1,0:T(8,128)(2,1)S(1)}, bf16[1,1,128,2048]{3,2,1,0:T(8,128)(2,1)}, u32[]{:S(2)}) copy-start(bf16[1,1,128,2048]{3,2,1,0:T(8,128)(2,1)} %get-tuple-element.550) | copy-start | bytes 1572868
  34.8 177.6 %all-gather.19.cloned.1.call-start = ((), (), s32[]{:S(2)}) async-start(), calls=%async_computation.4 | async-start | bytes 5242880 | tf_op jit(solution)/shard_map/all_gather | solution.py:10
  37.6 255.6 %all-gather.17.cloned.1.call-start = ((), (), s32[]{:S(2)}) async-start(), calls=%async_computation.3 | async-start | bytes 5242880 | tf_op jit(solution)/shard_map/all_gather | solution.py:10
  39.2 334.8 %all-gather.13.cloned.1.call-start = ((), (), s32[]{:S(2)}) async-start(), calls=%async_computation.1 | async-start | bytes 5242880 | tf_op jit(solution)/shard_map/all_gather | solution.py:10
  39.7 12.8 %copy-start.4 = (bf16[16,8,16,128]{3,2,1,0:T(8,128)(2,1)}, bf16[16,8,16,128]{3,2,1,0:T(8,128)(2,1)S(1)}, u32[]{:S(2)}) copy-start(bf16[16,8,16,128]{3,2,1,0:T(8,128)(2,1)S(1)} %copy.146) | copy-start | bytes 1572868
  41.0 11.5 %copy-start.2 = (bf16[16,8,16,128]{3,2,1,0:T(8,128)(2,1)}, bf16[16,8,16,128]{3,2,1,0:T(8,128)(2,1)S(1)}, u32[]{:S(2)}) copy-start(bf16[16,8,16,128]{3,2,1,0:T(8,128)(2,1)S(1)} %copy.147) | copy-start | bytes 1572868
  293.1 4.8 %copy-start.14 = (f32[16]{0:T(128)S(1)}, f32[16]{0:T(128)}, u32[]{:S(2)}) copy-start(f32[16]{0:T(128)} %param.27) | copy-start | bytes 196
  330.3 6.5 %copy-start.3 = (bf16[16,8,16,128]{3,2,1,0:T(8,128)(2,1)S(1)}, bf16[16,8,16,128]{3,2,1,0:T(8,128)(2,1)}, u32[]{:S(2)}) copy-start(bf16[16,8,16,128]{3,2,1,0:T(8,128)(2,1)} %copy-done.2) | copy-start | bytes 1572868
  334.9 39.2 %copy-start.1 = (f32[1,16,128,128]{3,2,1,0:T(8,128)S(1)}, f32[1,16,128,128]{3,2,1,0:T(8,128)}, u32[]{:S(2)}) copy-start(f32[1,16,128,128]{3,2,1,0:T(8,128)} %custom-call) | copy-start | bytes 3145732
  378.6 1.9 copy-start.5
  378.6 1.8 copy-start.7
  378.6 2.0 copy-start.8
  380.1 2.9 copy-start.9
Sparse Core Ops, SparseCore 0:
  20.2 29.3 all-gather.10
  51.2 80.2 all-gather.14
  133.1 79.2 all-gather.18
  213.8 79.2 all-gather.16
  294.5 79.5 all-gather.12
